TPU v7x, 256 devices: a whole 4x4x8 slice. The times are simulated.
256 devices in a mesh: sky: 8 (over z), chan: 32 (over x, y, core).
Axes of the slice: x: 4, y: 4, z: 8, core: 2. Of those that a mesh axis runs over, the one named last changes fastest.
Arguments:
- beam_images: float32 [32, 2, 288, 16384], P('sky', None, 'chan'), may hold values from -6 to 6
- beam_weights: float32 [32, 16384], P('sky'), may hold values from 0.05 to 1
- offsets: int32 [32], P('sky'), may hold values from 0 to 131071, as said below
Outputs:
- beam_residuals: float32 [32, 2, 288, 16384], P('sky', None, 'chan')
- depth_model: float32 [2, 512, 131072], P(None, None, ('sky', 'chan'))
Inputs may be any that keep to these rules, and one draw needn't show every extreme that they name: `offsets`: beam b starts in tile b // 4: its offset lies in [(b // 4) * 16384, (b // 4 + 1) * 16384).
All inputs are finite; a program needn't handle non-finite values.
Results may differ from a plain program's by a relative error of at most 0.00045.
Values sent between devices are 32-bit elements; how exact they have to be, the bound alone decides.
A program may use at most 128 MiB of HBM per device.

v0:
```python
import functools

import jax
import jax.numpy as jnp
import ml_dtypes
import numpy as np
from jax import lax
from jax.experimental import pallas as pl
from jax.experimental.pallas import tpu as pltpu
from jax.sharding import PartitionSpec as P

C = 288
F = 512
H = F // 2
BEAMS_DEV = 4
ITERS = 3
SKY = 8
CHAN = 32
PER = C // CHAN
MAIN = CHAN * 8
CHUNKS = 4

BAND_LOW = 800000000.0
BAND_WIDTH = 288000000.0
LIGHT = 299792458.0
DEPTH_STEP = 20.0
COMBINE_FLOOR = 0.5
THRESH_FRAC = 0.25
THRESH_BASE = 0.005
STEP_GAIN = 0.5
MESH = pl.DeviceIdType.MESH
F32 = jnp.float32
BF16 = jnp.bfloat16
VMEM_LIMIT = 56 << 20


def tables():
    one = np.float32
    channel = np.arange(C, dtype=one)
    freq = one(BAND_LOW) + (channel + one(0.5)) * one(BAND_WIDTH / C)
    lam = one(LIGHT) / freq
    lam_sq = lam * lam
    lam_sq = lam_sq - np.mean(lam_sq, dtype=one)
    depth = (H - np.arange(H, dtype=one)) * one(DEPTH_STEP)
    angle = (one(2.0) * depth)[:, None] * lam_sq[None, :]
    order = np.arange(C).reshape(CHAN, PER)
    order = np.concatenate([order[:, :8].reshape(-1), order[:, 8]])
    angle = angle[:, order].astype(np.float64)
    cosine, sine = np.cos(angle).astype(one), np.sin(angle).astype(one)

    def parts(value):
        high = value.astype(ml_dtypes.bfloat16)
        return high, (value - high.astype(one)).astype(ml_dtypes.bfloat16)

    extra = np.zeros((8, C), one)
    extra[0] = 1.0
    synth = np.concatenate([cosine, sine, extra], 0) / one(C)
    high, low = parts(synth)
    synth = np.concatenate([high[:, :MAIN], high[:, :MAIN], low[:, :MAIN], high[:, MAIN:], high[:, MAIN:], low[:, MAIN:]], 1)
    high, low = parts(np.concatenate([cosine.T, sine.T], 1))
    forward = np.concatenate([high, high, low], 1)
    turn = np.zeros((H, H), one)
    turn[np.arange(H), (-np.arange(H)) % H] = 1.0
    turn = np.concatenate([turn] * 3, 1).astype(ml_dtypes.bfloat16)
    return synth, forward, turn


def split(value):
    high = value.astype(BF16)
    return high, (value - high.astype(F32)).astype(BF16)


def dot(left, right):
    return jnp.dot(left, right, preferred_element_type=F32)


def sub_iota():
    return lax.broadcasted_iota(jnp.int32, (8, 128), 0)


def lane_iota():
    return lax.broadcasted_iota(jnp.int32, (8, 128), 1)


def swap_pairs(tiles):
    rows = sub_iota()
    low, even = rows < 4, (rows & 2) == 0
    a0, a1, a2, a3 = tiles
    b0 = jnp.where(low, a0, pltpu.roll(a2, 4, 0))
    b1 = jnp.where(low, a1, pltpu.roll(a3, 4, 0))
    b2 = jnp.where(low, pltpu.roll(a0, 4, 0), a2)
    b3 = jnp.where(low, pltpu.roll(a1, 4, 0), a3)
    return (
        jnp.where(even, b0, pltpu.roll(b1, 2, 0)),
        jnp.where(even, pltpu.roll(b0, 6, 0), b1),
        jnp.where(even, b2, pltpu.roll(b3, 2, 0)),
        jnp.where(even, pltpu.roll(b2, 6, 0), b3),
    )


def pair_rows(rows8, first):
    rows = sub_iota()
    row = [jnp.broadcast_to(rows8[first + k : first + k + 1], (8, 128)) for k in range(4)]
    return jnp.where(rows < 4, jnp.where(rows < 2, row[0], row[1]), jnp.where(rows < 6, row[2], row[3]))


def combine_kernel(start_ref, x_ref, x9_ref, w_ref, o_ref, o9_ref, ow_ref):
    beam = pl.program_id(0)

    @pl.when(beam == 0)
    def _():
        o_ref[...] = jnp.zeros_like(o_ref)
        o9_ref[...] = jnp.zeros_like(o9_ref)
        ow_ref[...] = jnp.zeros_like(ow_ref)

    start = start_ref[beam]
    whole, shift = start // 128, start % 128
    tile, part = whole // 4, (whole % 4) * 2
    lanes, rows = lane_iota(), sub_iota()
    stays = lanes >= shift
    below = rows >= part
    zero = jnp.zeros((8, 128), F32)

    def add_narrow(at, value, last_shift, last_turn, ref):
        rolled = pltpu.roll(value, shift, 1)
        moved = pltpu.roll(rolled, 2, 0)
        joined = jnp.where(stays, rolled, jnp.where(rows >= 2, moved, last_shift))
        turned = pltpu.roll(joined, part, 0)
        ref[at] += jnp.where(below, turned, last_turn)
        return moved, turned

    def step(i, carry):
        last, narrow9, narrow_w = carry
        weights = w_ref[0, pl.ds(pl.multiple_of(i * 8, 8), 8), :]
        for half in range(2):
            at = i * 2 + half
            row = pl.ds(pl.multiple_of(at * 8, 8), 8)
            pair = pair_rows(weights, half * 4)
            narrow9 = add_narrow(tile + at, x9_ref[0, 0, row, :] * pair, *narrow9, o9_ref)
            narrow_w = add_narrow(tile + at, pair, *narrow_w, ow_ref)
            blocks = [swap_pairs([x_ref[0, 4 * g + k, row, :] for k in range(4)]) for g in range(2)]
            for k in range(4):
                weight = jnp.broadcast_to(weights[half * 4 + k : half * 4 + k + 1], (8, 128))
                rolled = [pltpu.roll(blocks[g][k] * weight, shift, 1) for g in range(2)]
                for g in range(2):
                    o_ref[whole + at * 4 + k, 8 * g : 8 * g + 8] += jnp.where(stays, rolled[g], last[g])
                last = rolled
        return last, narrow9, narrow_w

    last, narrow9, narrow_w = lax.fori_loop(0, 16, step, ([zero, zero], (zero, zero), (zero, zero)))
    for g in range(2):
        o_ref[whole + 128, 8 * g : 8 * g + 8] += jnp.where(stays, 0.0, last[g])
    add_narrow(tile + 32, zero, *narrow9, o9_ref)
    add_narrow(tile + 32, zero, *narrow_w, ow_ref)


def gather_kernel(start_ref, r_ref, r9_ref, w_ref, o_ref):
    beam = pl.program_id(0)
    start = start_ref[beam]
    end = start_ref[BEAMS_DEV]
    whole, shift = start // 128, start % 128
    tile, part = whole // 4, (whole % 4) * 2
    lanes, rows = lane_iota(), sub_iota()
    stays = lanes < 128 - shift
    above = rows < 8 - part
    back = (128 - shift) % 128
    turn = (8 - part) % 8

    def block(at, g):
        value = r_ref[at, 8 * g : 8 * g + 8]
        return pltpu.roll(jnp.where(at < end, value, 0.0), back, 1)

    def turned9(at):
        return pltpu.roll(jnp.where(at * 4 < end, r9_ref[at], 0.0), turn, 0)

    def rolled9(first, second):
        return pltpu.roll(jnp.where(above, first, second), back, 1)

    first = turned9(tile)
    second = turned9(tile + 1)

    def step(i, carry):
        now, rolled, turned = carry
        weights = w_ref[0, pl.ds(pl.multiple_of(i * 8, 8), 8), :]
        for half in range(2):
            at = i * 2 + half
            row = pl.ds(pl.multiple_of(at * 8, 8), 8)
            beyond = turned9(jnp.minimum(tile + at + 2, 63))
            after = rolled9(turned, beyond)
            moved = jnp.where(rows < 6, pltpu.roll(rolled, 6, 0), pltpu.roll(after, 6, 0))
            o_ref[0, 8, row, :] = jnp.where(stays, rolled, moved) * pair_rows(weights, half * 4)
            rolled, turned = after, beyond
            results = [[], []]
            for k in range(4):
                weight = jnp.broadcast_to(weights[half * 4 + k : half * 4 + k + 1], (8, 128))
                later = [block(whole + at * 4 + k + 1, g) for g in range(2)]
                for g in range(2):
                    results[g].append(jnp.where(stays, now[g], later[g]) * weight)
                now = later
            for g in range(2):
                for k, value in enumerate(swap_pairs(results[g])):
                    o_ref[0, 4 * g + k, row, :] = value
        return now, rolled, turned

    lax.fori_loop(0, 16, step, ([block(whole, g) for g in range(2)], rolled9(first, second), second))


def exchange_kernel(
    num, num9, wsum, synth, forward, turn, res, res9, depth,
    hx, hx9, hw, sb, sb9, rx, rx9, bk, bk9, flat, rhs_c, rhs_f, model_re, model_im,
    up_send, up_recv, up9_send, up9_recv, upw_send, upw_recv,
    to_send, to_recv, to9_send, to9_recv,
    back_send, back_recv, back9_send, back9_recv,
    down_send, down_recv, down9_send, down9_recv,
):
    sky, me = lax.axis_index("sky"), lax.axis_index("chan")
    up, down = lax.rem(sky + 1, SKY), lax.rem(sky + SKY - 1, SKY)
    mine = pl.ds(pl.multiple_of(me * 8, 8), 8)

    barrier = pltpu.get_barrier_semaphore()

    def greet(d, carry):
        pl.semaphore_signal(barrier, inc=1, device_id=(sky, lax.rem(me + d, CHAN)), device_id_type=MESH)
        return carry

    lax.fori_loop(1, CHAN, greet, 0)
    for other in (up, down):
        pl.semaphore_signal(barrier, inc=1, device_id=(other, me), device_id_type=MESH)
    pl.semaphore_wait(barrier, CHAN + 1)

    def remote(src, dst, send, recv, device):
        return pltpu.make_async_remote_copy(
            src_ref=src, dst_ref=dst, send_sem=send, recv_sem=recv, device_id=device, device_id_type=MESH
        )

    second = pl.ds(CHAN, CHAN)
    first = pl.ds(0, CHAN)
    up_w = remote(wsum.at[CHAN + me], hw, upw_send, upw_recv, (up, me))
    up_9 = remote(num9.at[second], hx9, up9_send, up9_recv, (up, me))

    def up_copy(s):
        return remote(num.at[second, s], hx.at[:, s], up_send.at[s], up_recv.at[s], (up, me))

    def down_copy(s):
        return remote(res.at[first, s], res.at[second, s], down_send.at[s], down_recv.at[s], (down, me))

    down_9 = remote(res9.at[first], res9.at[second], down9_send, down9_recv, (down, me))

    up_copy(0).start()
    up_9.start()
    up_w.start()
    for s in range(1, CHUNKS):
        up_copy(s).start()

    def spread(s):
        up_copy(s).wait_recv()
        sb[s] = num[:CHAN, s] + jnp.where(sky > 0, hx[:, s], 0.0)
        pltpu.make_async_copy(sb.at[s, me], rx.at[s, me], to_recv.at[s]).start()

        def send(d, carry):
            to = lax.rem(me + d, CHAN)
            remote(sb.at[s, to], rx.at[s, me], to_send.at[s], to_recv.at[s], (sky, to)).start()
            return carry

        lax.fori_loop(1, CHAN, send, 0)

    def spread9():
        up_9.wait_recv()
        up_w.wait_recv()
        sb9[...] = num9[:CHAN] + jnp.where(sky > 0, hx9[...], 0.0)
        pltpu.make_async_copy(sb9.at[me], rx9.at[mine], to9_recv).start()

        def send(d, carry):
            to = lax.rem(me + d, CHAN)
            remote(sb9.at[to], rx9.at[mine], to9_send, to9_recv, (sky, to)).start()
            return carry

        lax.fori_loop(1, CHAN, send, 0)

    is_zero = lax.broadcasted_iota(jnp.int32, (H, 128), 0) == 0

    def synthesis(field):
        high, low = split(field)
        rhs_c[0:MAIN] = high[:MAIN]
        rhs_c[MAIN : 2 * MAIN] = low[:MAIN]
        rhs_c[2 * MAIN : 3 * MAIN] = high[:MAIN]
        rhs_c[3 * MAIN : 3 * MAIN + 32] = high[MAIN:]
        rhs_c[3 * MAIN + 32 : 3 * MAIN + 64] = low[MAIN:]
        rhs_c[3 * MAIN + 64 : 3 * MAIN + 96] = high[MAIN:]
        out = dot(synth[...], rhs_c[...])
        cos_q, cos_u = out[:H, :128], out[:H, 128:]
        sin_q, sin_u = out[H:F, :128], out[H:F, 128:]
        plus_re = jnp.where(is_zero, out[F : F + 1, :128], cos_q + sin_u)
        plus_im = jnp.where(is_zero, out[F : F + 1, 128:], cos_u - sin_q)
        return plus_re, plus_im, cos_q - sin_u, cos_u + sin_q

    def residual():
        plus_re, plus_im = model_re[:H], model_im[:H]
        minus_re, minus_im = model_re[H:], model_im[H:]
        zero_re, zero_im = plus_re[0:1], plus_im[0:1]
        plus_re = jnp.where(is_zero, 0.0, plus_re)
        plus_im = jnp.where(is_zero, 0.0, plus_im)

        def put(value, row, column):
            high, low = split(value)
            columns = slice(column, column + 128)
            rhs_f[row : row + H, columns] = high
            rhs_f[F + row : F + row + H, columns] = low
            rhs_f[2 * F + row : 2 * F + row + H, columns] = high

        put(plus_re + minus_re, 0, 0)
        put(plus_im + minus_im, 0, 128)
        put(minus_im - plus_im, H, 0)
        put(plus_re - minus_re, H, 128)
        seen = dot(forward[...], rhs_f[...])
        return flat[...] - (seen + jnp.concatenate([zero_re, zero_im], 1))

    def deconvolve(s):
        pltpu.make_async_copy(rx.at[s], rx.at[s], to_recv.at[s]).wait()
        scale = wsum[me] + jnp.where(sky > 0, hw[...], 0.0) + COMBINE_FLOOR
        rows = lax.broadcasted_iota(jnp.int32, (8, 128), 0)
        scale = 1.0 / jnp.sum(jnp.where(rows == 2 * s, scale, 0.0), axis=0, keepdims=True)
        for q in range(2):
            columns = slice(128 * q, 128 * q + 128)
            flat[:MAIN, columns] = rx[s, :, pl.ds(q, 8, stride=2), :].reshape(MAIN, 128) * scale
            flat[MAIN:, columns] = rx9[pl.ds(2 * s + q, CHAN, stride=8), :] * scale
        dirty = synthesis(flat[...])
        re = jnp.concatenate([dirty[0], dirty[2]], 0)
        im = jnp.concatenate([dirty[1], dirty[3]], 0)
        mag = jnp.sqrt(re * re + im * im)
        thresh = THRESH_FRAC * jnp.max(mag, axis=0, keepdims=True) + THRESH_BASE
        mag = STEP_GAIN * mag
        factor = STEP_GAIN * (jnp.maximum(mag - thresh, 0.0) / jnp.maximum(mag, thresh))
        model_re[...] = re * factor
        model_im[...] = im * factor

        def iteration(_, carry):
            grown = synthesis(residual())
            for plus in range(2):
                part = slice(H * plus, H * plus + H)
                re = model_re[part] + STEP_GAIN * grown[2 * plus]
                im = model_im[part] + STEP_GAIN * grown[2 * plus + 1]
                mag = jnp.sqrt(re * re + im * im)
                factor = jnp.maximum(mag - thresh, 0.0) / jnp.maximum(mag, thresh)
                model_re[part] = re * factor
                model_im[part] = im * factor
            return carry

        lax.fori_loop(0, ITERS - 1, iteration, 0)
        rest = residual()
        for q in range(2):
            columns = slice(128 * q, 128 * q + 128)
            bk[s, :, pl.ds(q, 8, stride=2), :] = rest[:MAIN, columns].reshape(CHAN, 8, 128)
            bk9[pl.ds(2 * s + q, CHAN, stride=8), :] = rest[MAIN:, columns]
        pltpu.make_async_copy(bk.at[s, me], res.at[me, s], back_recv.at[s]).start()

        def send(d, carry):
            to = lax.rem(me + d, CHAN)
            remote(bk.at[s, to], res.at[me, s], back_send.at[s], back_recv.at[s], (sky, to)).start()
            return carry

        lax.fori_loop(1, CHAN, send, 0)

        lanes = pl.ds(pl.multiple_of(s * 128, 128), 128)
        depth[0, 0:H, lanes] = model_re[H:]
        depth[1, 0:H, lanes] = model_im[H:]
        plus = jnp.concatenate([model_re[:H], model_im[:H]], 1)
        high = plus.astype(BF16)
        plus = plus - high.astype(F32)
        middle = plus.astype(BF16)
        low = (plus - middle.astype(F32)).astype(BF16)
        rhs_f[0:H] = high
        rhs_f[H : 2 * H] = middle
        rhs_f[2 * H : 3 * H] = low
        turned = dot(turn[...], rhs_f[0 : 3 * H])
        depth[0, H:, lanes] = turned[:, :128]
        depth[1, H:, lanes] = turned[:, 128:]

    def send_back9():
        pltpu.make_async_copy(bk9.at[mine], res9.at[me], back9_recv).start()

        def send(d, carry):
            to = lax.rem(me + d, CHAN)
            row = pl.ds(pl.multiple_of(to * 8, 8), 8)
            remote(bk9.at[row], res9.at[me], back9_send, back9_recv, (sky, to)).start()
            return carry

        lax.fori_loop(1, CHAN, send, 0)

    def step(i, carry):
        @pl.when(i < CHUNKS)
        def _():
            spread(i)

        @pl.when(i == 0)
        def _():
            spread9()

        @pl.when(i == 1)
        def _():
            pltpu.make_async_copy(rx9, rx9, to9_recv).wait()

        @pl.when((i >= 1) & (i <= CHUNKS))
        def _():
            deconvolve(i - 1)

        @pl.when(i == CHUNKS)
        def _():
            send_back9()

        @pl.when(i >= 2)
        def _():
            s = i - 2
            pltpu.make_async_copy(bk.at[s], bk.at[s], back_recv.at[s]).wait()
            down_copy(s).start()

        return carry

    lax.fori_loop(0, CHUNKS + 2, step, 0)
    pltpu.make_async_copy(hx9, hx9, back9_recv).wait()
    down_9.start()

    others = pl.ds(0, CHAN - 1)
    up_w.wait_send()
    up_9.wait_send()
    for s in range(CHUNKS):
        up_copy(s).wait_send()
        pltpu.make_async_copy(sb.at[s, others], sb.at[s, others], to_send.at[s]).wait()
        pltpu.make_async_copy(sb.at[s, others], sb.at[s, others], back_send.at[s]).wait()
    pltpu.make_async_copy(sb9.at[others], sb9.at[others], to9_send).wait()
    pltpu.make_async_copy(sb9.at[others], sb9.at[others], back9_send).wait()
    for s in range(CHUNKS):
        down_copy(s).wait()
    down_9.wait()


def body(beam_images, beam_weights, offsets):
    synth, forward, turn = tables()
    sky = lax.axis_index("sky")
    start = offsets - sky * (CHAN * F)
    end = jnp.where(sky == SKY - 1, CHAN * CHUNKS, 2 * CHAN * CHUNKS)
    start = jnp.concatenate([start, jnp.broadcast_to(end, (1,)).astype(jnp.int32)])
    images = beam_images.reshape(4, 2, PER, 128, 128).transpose(0, 2, 3, 1, 4).reshape(4, PER, 256, 128)
    weights = beam_weights.reshape(4, 128, 128)
    shape = jax.ShapeDtypeStruct

    num, num9, wsum = pl.pallas_call(
        combine_kernel,
        grid_spec=pltpu.PrefetchScalarGridSpec(
            num_scalar_prefetch=1,
            grid=(BEAMS_DEV,),
            in_specs=[
                pl.BlockSpec((1, 8, 256, 128), lambda b, _: (b, 0, 0, 0)),
                pl.BlockSpec((1, 1, 256, 128), lambda b, _: (b, 8, 0, 0)),
                pl.BlockSpec((1, 128, 128), lambda b, _: (b, 0, 0)),
            ],
            out_specs=[
                pl.BlockSpec((256, 16, 128), lambda b, _: (0, 0, 0)),
                pl.BlockSpec((64, 8, 128), lambda b, _: (0, 0, 0)),
                pl.BlockSpec((64, 8, 128), lambda b, _: (0, 0, 0)),
            ],
        ),
        out_shape=[shape((256, 16, 128), F32), shape((64, 8, 128), F32), shape((64, 8, 128), F32)],
        compiler_params=pltpu.CompilerParams(vmem_limit_bytes=VMEM_LIMIT),
    )(start, images, images, weights)

    dma = pltpu.SemaphoreType.DMA
    vmem = pltpu.VMEM
    whole = pl.BlockSpec(memory_space=vmem)
    res, res9, depth = pl.pallas_call(
        exchange_kernel,
        in_specs=[whole] * 6,
        out_specs=[whole] * 3,
        out_shape=[
            shape((2 * CHAN, CHUNKS, 16, 128), F32),
            shape((2 * CHAN, 8, 128), F32),
            shape((2, F, F), F32),
        ],
        scratch_shapes=[
            vmem((CHAN, CHUNKS, 16, 128), F32),
            vmem((CHAN, 8, 128), F32),
            vmem((8, 128), F32),
            vmem((CHUNKS, CHAN, 16, 128), F32),
            vmem((CHAN, 8, 128), F32),
            vmem((CHUNKS, CHAN, 16, 128), F32),
            vmem((CHAN * 8, 128), F32),
            vmem((CHUNKS, CHAN, 16, 128), F32),
            vmem((CHAN * 8, 128), F32),
            vmem((C, 256), F32),
            vmem((3 * C, 256), BF16),
            vmem((3 * F, 256), BF16),
            vmem((F, 128), F32),
            vmem((F, 128), F32),
            dma((CHUNKS,)), dma((CHUNKS,)), dma, dma, dma, dma,
            dma((CHUNKS,)), dma((CHUNKS,)), dma, dma,
            dma((CHUNKS,)), dma((CHUNKS,)), dma, dma,
            dma((CHUNKS,)), dma((CHUNKS,)), dma, dma,
        ],
        compiler_params=pltpu.CompilerParams(collective_id=0, has_side_effects=True, vmem_limit_bytes=VMEM_LIMIT),
    )(num.reshape(2 * CHAN, CHUNKS, 16, 128), num9, wsum, jnp.asarray(synth), jnp.asarray(forward), jnp.asarray(turn))

    out = pl.pallas_call(
        gather_kernel,
        grid_spec=pltpu.PrefetchScalarGridSpec(
            num_scalar_prefetch=1,
            grid=(BEAMS_DEV,),
            in_specs=[
                pl.BlockSpec((256, 16, 128), lambda b, _: (0, 0, 0)),
                pl.BlockSpec((64, 8, 128), lambda b, _: (0, 0, 0)),
                pl.BlockSpec((1, 128, 128), lambda b, _: (b, 0, 0)),
            ],
            out_specs=pl.BlockSpec((1, PER, 256, 128), lambda b, _: (b, 0, 0, 0)),
        ),
        out_shape=shape((BEAMS_DEV, PER, 256, 128), F32),
        compiler_params=pltpu.CompilerParams(vmem_limit_bytes=VMEM_LIMIT),
    )(start, res.reshape(256, 16, 128), res9, weights)
    out = out.reshape(4, PER, 128, 2, 128).transpose(0, 3, 1, 2, 4).reshape(4, 2, PER, 128 * 128)
    return out, depth


def solution(mesh):
    return jax.shard_map(
        body,
        mesh=mesh,
        in_specs=(P("sky", None, "chan", None), P("sky", None), P("sky")),
        out_specs=(P("sky", None, "chan", None), P(None, None, ("sky", "chan"))),
        check_vma=False,
    )
```

profile of v0, /device:TPU:1, one launch (start us, length us, event | category | flops | bytes accessed | tf_op | source)
XLA Modules:
  0.0 96.1 jit_solution(6734580685617956712)
XLA Ops:
  0.6 0.7 broadcast_subtract_fusion
  1.3 0.6 pad_add_fusion.start_ref
  1.9 1.7 %copy.12 = f32[1,4,128,128]{3,2,1,0:T(8,128)} copy(f32[1,4,128,128]{3,1,2,0:T(4,128)} %bitcast.24) | data formatting | bytes 524288
  3.5 10.0 %shard_map.77 = (f32[256,16,128]{2,1,0:T(8,128)}, f32[64,8,128]{2,1,0:T(8,128)}, f32[64,8,128]{2,1,0:T(8,128)}) custom-call(s32[5]{0:T(128)} %pad_add_fusion.start_ref, f32[4,9,256,128]{3,2,1,0:T(8,128)} %bitcast.17, f32[4,9,256,128]{3,2,1,0:T(8,128)} %bitcast.18, f32[4,128,128]{2,1,0:T(8,128)} %bitcast.20), custom_call_target="tpu_custom_call" | custom-call | tf_op jit(solution)/shard_map/pallas_call | solution.py:447
  13.5 71.4 %shard_map.78 = (f32[64,4,16,128]{3,2,1,0:T(8,128)}, f32[64,8,128]{2,1,0:T(8,128)}, f32[2,512,512]{2,1,0:T(8,128)}) custom-call(f32[64,4,16,128]{3,2,1,0:T(8,128)} %bitcast.22, f32[64,8,128]{2,1,0:T(8,128)} %get-tuple-element.9.num9, f32[64,8,128]{2,1,0:T(8,128)} %get-tuple-element.10.wsum, bf16[520,864]{1,0:T(8,128)(2,1)} %constant.20.clone.synth, ...), custom_call_target="tpu_custom_call" | custom-call | tf_op jit(solution)/shard_map/pallas_call | solution.py:470
  85.0 0.0 copy-start
  85.0 9.8 %shard_map.79 = f32[4,9,256,128]{3,2,1,0:T(8,128)} custom-call(s32[5]{0:T(128)} %pad_add_fusion.start_ref, f32[256,16,128]{2,1,0:T(8,128)} %bitcast.23, f32[64,8,128]{2,1,0:T(8,128)} %get-tuple-element.12.r9_ref, f32[4,128,128]{2,1,0:T(8,128)} %bitcast.21), custom_call_target="tpu_custom_call" | custom-call | tf_op jit(solution)/shard_map/pallas_call | solution.py:502
  94.7 0.0 copy-done
  94.8 1.3 %copy.14 = f32[2,512,512]{2,1,0:T(8,128)} copy(f32[2,512,512]{2,1,0:T(8,128)S(1)} %copy-done) | data formatting | bytes 4194304
Async XLA Ops:
  85.0 9.8 %copy-start = (f32[2,512,512]{2,1,0:T(8,128)S(1)}, f32[2,512,512]{2,1,0:T(8,128)}, u32[]{:S(2)}) copy-start(f32[2,512,512]{2,1,0:T(8,128)} %get-tuple-element.17) | copy-start | bytes 6291460
where the time goes:
time: 96.3 us; the launch traced here: 96.1 us
  Pallas kernels  91.2 us (95%)
  local copies, waits for them, and re-layouts  2.98 us (3%)
  other arithmetic  1.24 us (1%)
    pallas_call x1, Pallas kernels, body(): pl.pallas_call(exchange_kernel, in_specs=[whole] * 6, out_specs=[whole] *...  71.4 us
    pallas_call x1, Pallas kernels, body(): pl.pallas_call(combine_kernel, grid_spec=pltpu.PrefetchScalarGridSpec(num...  9.97 us
    pallas_call x1, Pallas kernels, body(): pl.pallas_call(gather_kernel, grid_spec=pltpu.PrefetchScalarGridSpec(num_...  9.78 us
    unnamed x4, local copies, waits for them, and re-layouts  2.98 us

commit v1 on v0

--- a/solution.py
+++ b/solution.py
@@ -32,6 +32,9 @@
 F32 = jnp.float32
 BF16 = jnp.bfloat16
 VMEM_LIMIT = 56 << 20
+UNROLL = 8
+STRAIGHT_UP = ()
+STRAIGHT_DOWN = (3,)
 
 
 def tables():
@@ -98,13 +101,25 @@
     )
 
 
-def pair_rows(rows8, first):
-    rows = sub_iota()
-    row = [jnp.broadcast_to(rows8[first + k : first + k + 1], (8, 128)) for k in range(4)]
-    return jnp.where(rows < 4, jnp.where(rows < 2, row[0], row[1]), jnp.where(rows < 6, row[2], row[3]))
-
-
-def combine_kernel(start_ref, x_ref, x9_ref, w_ref, o_ref, o9_ref, ow_ref):
+def beam_start(offsets_ref, beam):
+    return offsets_ref[beam] - lax.axis_index("sky") * (CHAN * F)
+
+
+def weight_rows(w_ref, i, beam):
+    back = lax.rem(8 - beam, 8)
+    rows = []
+    for k in range(4):
+        two = pltpu.roll(w_ref[pl.ds(pl.multiple_of(i * 32 + k * 8, 8), 8), :], back, 0)
+        rows += [jnp.broadcast_to(two[r : r + 1], (8, 128)) for r in (0, 4)]
+    return rows
+
+
+def pair_rows(rows):
+    at = sub_iota()
+    return jnp.where(at < 4, jnp.where(at < 2, rows[0], rows[1]), jnp.where(at < 6, rows[2], rows[3]))
+
+
+def combine_kernel(offsets_ref, x_ref, x9_ref, w_ref, o_ref, o9_ref, ow_ref):
     beam = pl.program_id(0)
 
     @pl.when(beam == 0)
@@ -113,7 +128,7 @@
         o9_ref[...] = jnp.zeros_like(o9_ref)
         ow_ref[...] = jnp.zeros_like(ow_ref)
 
-    start = start_ref[beam]
+    start = beam_start(offsets_ref, beam)
     whole, shift = start // 128, start % 128
     tile, part = whole // 4, (whole % 4) * 2
     lanes, rows = lane_iota(), sub_iota()
@@ -121,43 +136,49 @@
     below = rows >= part
     zero = jnp.zeros((8, 128), F32)
 
-    def add_narrow(at, value, last_shift, last_turn, ref):
+    def narrow(value, last_shift, last_turn):
         rolled = pltpu.roll(value, shift, 1)
         moved = pltpu.roll(rolled, 2, 0)
         joined = jnp.where(stays, rolled, jnp.where(rows >= 2, moved, last_shift))
         turned = pltpu.roll(joined, part, 0)
-        ref[at] += jnp.where(below, turned, last_turn)
-        return moved, turned
+        return jnp.where(below, turned, last_turn), (moved, turned)
 
     def step(i, carry):
-        last, narrow9, narrow_w = carry
-        weights = w_ref[0, pl.ds(pl.multiple_of(i * 8, 8), 8), :]
+        last, carry9, carry_w = carry
+        blocks_at, tiles_at = pl.ds(whole + i * 8, 8), pl.ds(tile + i * 2, 2)
+        weights = weight_rows(w_ref, i, beam)
+        wide, thin, thin_w = [], [], []
         for half in range(2):
-            at = i * 2 + half
-            row = pl.ds(pl.multiple_of(at * 8, 8), 8)
-            pair = pair_rows(weights, half * 4)
-            narrow9 = add_narrow(tile + at, x9_ref[0, 0, row, :] * pair, *narrow9, o9_ref)
-            narrow_w = add_narrow(tile + at, pair, *narrow_w, ow_ref)
+            row = pl.ds(pl.multiple_of((i * 2 + half) * 8, 8), 8)
+            pair = pair_rows(weights[half * 4 : half * 4 + 4])
+            added, carry9 = narrow(x9_ref[0, 0, row, :] * pair, *carry9)
+            thin.append(added)
+            added, carry_w = narrow(pair, *carry_w)
+            thin_w.append(added)
             blocks = [swap_pairs([x_ref[0, 4 * g + k, row, :] for k in range(4)]) for g in range(2)]
             for k in range(4):
-                weight = jnp.broadcast_to(weights[half * 4 + k : half * 4 + k + 1], (8, 128))
-                rolled = [pltpu.roll(blocks[g][k] * weight, shift, 1) for g in range(2)]
-                for g in range(2):
-                    o_ref[whole + at * 4 + k, 8 * g : 8 * g + 8] += jnp.where(stays, rolled[g], last[g])
+                rolled = [pltpu.roll(blocks[g][k] * weights[half * 4 + k], shift, 1) for g in range(2)]
+                wide.append(jnp.concatenate([jnp.where(stays, rolled[g], last[g]) for g in range(2)], 0))
                 last = rolled
-        return last, narrow9, narrow_w
-
-    last, narrow9, narrow_w = lax.fori_loop(0, 16, step, ([zero, zero], (zero, zero), (zero, zero)))
+        o_ref[blocks_at] += jnp.stack(wide)
+        o9_ref[tiles_at] += jnp.stack(thin)
+        ow_ref[tiles_at] += jnp.stack(thin_w)
+        return last, carry9, carry_w
+
+    last, carry9, carry_w = lax.fori_loop(
+        0, 16, step, ([zero, zero], (zero, zero), (zero, zero)), unroll=UNROLL
+    )
     for g in range(2):
         o_ref[whole + 128, 8 * g : 8 * g + 8] += jnp.where(stays, 0.0, last[g])
-    add_narrow(tile + 32, zero, *narrow9, o9_ref)
-    add_narrow(tile + 32, zero, *narrow_w, ow_ref)
-
-
-def gather_kernel(start_ref, r_ref, r9_ref, w_ref, o_ref):
+    o9_ref[tile + 32] += narrow(zero, *carry9)[0]
+    ow_ref[tile + 32] += narrow(zero, *carry_w)[0]
+
+
+def gather_kernel(offsets_ref, r_ref, r9_ref, w_ref, d_ref, o_ref, od_ref):
     beam = pl.program_id(0)
-    start = start_ref[beam]
-    end = start_ref[BEAMS_DEV]
+    start = beam_start(offsets_ref, beam)
+    tail = lax.axis_index("sky") == SKY - 1
+    end = jnp.where(tail, CHAN * CHUNKS, 2 * CHAN * CHUNKS)
     whole, shift = start // 128, start % 128
     tile, part = whole // 4, (whole % 4) * 2
     lanes, rows = lane_iota(), sub_iota()
@@ -181,37 +202,38 @@
 
     def step(i, carry):
         now, rolled, turned = carry
-        weights = w_ref[0, pl.ds(pl.multiple_of(i * 8, 8), 8), :]
+        weights = weight_rows(w_ref, i, beam)
         for half in range(2):
             at = i * 2 + half
             row = pl.ds(pl.multiple_of(at * 8, 8), 8)
             beyond = turned9(jnp.minimum(tile + at + 2, 63))
             after = rolled9(turned, beyond)
             moved = jnp.where(rows < 6, pltpu.roll(rolled, 6, 0), pltpu.roll(after, 6, 0))
-            o_ref[0, 8, row, :] = jnp.where(stays, rolled, moved) * pair_rows(weights, half * 4)
+            o_ref[0, 8, row, :] = jnp.where(stays, rolled, moved) * pair_rows(weights[half * 4 : half * 4 + 4])
             rolled, turned = after, beyond
             results = [[], []]
             for k in range(4):
-                weight = jnp.broadcast_to(weights[half * 4 + k : half * 4 + k + 1], (8, 128))
                 later = [block(whole + at * 4 + k + 1, g) for g in range(2)]
                 for g in range(2):
-                    results[g].append(jnp.where(stays, now[g], later[g]) * weight)
+                    results[g].append(jnp.where(stays, now[g], later[g]) * weights[half * 4 + k])
                 now = later
             for g in range(2):
                 for k, value in enumerate(swap_pairs(results[g])):
                     o_ref[0, 4 * g + k, row, :] = value
         return now, rolled, turned
 
-    lax.fori_loop(0, 16, step, ([block(whole, g) for g in range(2)], rolled9(first, second), second))
+    init = ([block(whole, g) for g in range(2)], rolled9(first, second), second)
+    lax.fori_loop(0, 16, step, init, unroll=UNROLL)
+    od_ref[...] = d_ref[...]
 
 
 def exchange_kernel(
     num, num9, wsum, synth, forward, turn, res, res9, depth,
-    hx, hx9, hw, sb, sb9, rx, rx9, bk, bk9, flat, rhs_c, rhs_f, model_re, model_im,
+    hx, hx9, hw, sb, sb9, rx, rx_up, rx9, bk, bk9, flat, rhs_c, rhs_f, model_re, model_im,
     up_send, up_recv, up9_send, up9_recv, upw_send, upw_recv,
     to_send, to_recv, to9_send, to9_recv,
     back_send, back_recv, back9_send, back9_recv,
-    down_send, down_recv, down9_send, down9_recv,
+    down_send, down_recv, down9_send, down9_recv, ready,
 ):
     sky, me = lax.axis_index("sky"), lax.axis_index("chan")
     up, down = lax.rem(sky + 1, SKY), lax.rem(sky + SKY - 1, SKY)
@@ -227,6 +249,7 @@
     for other in (up, down):
         pl.semaphore_signal(barrier, inc=1, device_id=(other, me), device_id_type=MESH)
     pl.semaphore_wait(barrier, CHAN + 1)
+    pl.semaphore_signal(ready, inc=1, device_id=(down, me), device_id_type=MESH)
 
     def remote(src, dst, send, recv, device):
         return pltpu.make_async_remote_copy(
@@ -234,35 +257,52 @@
         )
 
     second = pl.ds(CHAN, CHAN)
-    first = pl.ds(0, CHAN)
     up_w = remote(wsum.at[CHAN + me], hw, upw_send, upw_recv, (up, me))
     up_9 = remote(num9.at[second], hx9, up9_send, up9_recv, (up, me))
 
     def up_copy(s):
         return remote(num.at[second, s], hx.at[:, s], up_send.at[s], up_recv.at[s], (up, me))
 
+    first = pl.ds(0, CHAN)
+    all_sent = pl.ds(0, CHAN - 1)
+
     def down_copy(s):
         return remote(res.at[first, s], res.at[second, s], down_send.at[s], down_recv.at[s], (down, me))
 
-    down_9 = remote(res9.at[first], res9.at[second], down9_send, down9_recv, (down, me))
-
-    up_copy(0).start()
+    def among(s, chunks):
+        return functools.reduce(jnp.logical_or, [s == k for k in chunks], s < 0)
+
+    def to_all(copies):
+        def send(d, carry):
+            to = lax.rem(me + d, CHAN)
+            for src, dst, send_sem, recv_sem, row in copies:
+                remote(src(to), dst, send_sem, recv_sem, (row, to)).start()
+            return carry
+
+        lax.fori_loop(1, CHAN, send, 0)
+
+    relayed = [s for s in range(CHUNKS) if s not in STRAIGHT_UP]
+    up_copy(relayed[0]).start()
     up_9.start()
     up_w.start()
-    for s in range(1, CHUNKS):
+    for s in relayed[1:]:
         up_copy(s).start()
 
     def spread(s):
-        up_copy(s).wait_recv()
-        sb[s] = num[:CHAN, s] + jnp.where(sky > 0, hx[:, s], 0.0)
-        pltpu.make_async_copy(sb.at[s, me], rx.at[s, me], to_recv.at[s]).start()
-
-        def send(d, carry):
-            to = lax.rem(me + d, CHAN)
-            remote(sb.at[s, to], rx.at[s, me], to_send.at[s], to_recv.at[s], (sky, to)).start()
-            return carry
-
-        lax.fori_loop(1, CHAN, send, 0)
+        @pl.when(jnp.logical_not(among(s, STRAIGHT_UP)))
+        def _():
+            up_copy(s).wait_recv()
+            sb[s] = num[:CHAN, s] + jnp.where(sky > 0, hx[:, s], 0.0)
+            pltpu.make_async_copy(sb.at[s, me], rx.at[s, me], to_recv.at[s]).start()
+            to_all([(lambda to: sb.at[s, to], rx.at[s, me], to_send.at[s], to_recv.at[s], sky)])
+
+    def straight_own(s):
+        pltpu.make_async_copy(num.at[me, s], rx.at[s, me], to_recv.at[s]).start()
+        to_all([(lambda to: num.at[to, s], rx.at[s, me], to_send.at[s], to_recv.at[s], sky)])
+
+    def straight_up(s):
+        remote(num.at[CHAN + me, s], rx_up.at[s, me], up_send.at[s], up_recv.at[s], (up, me)).start()
+        to_all([(lambda to: num.at[CHAN + to, s], rx_up.at[s, me], up_send.at[s], up_recv.at[s], up)])
 
     def spread9():
         up_9.wait_recv()
@@ -270,12 +310,7 @@
         sb9[...] = num9[:CHAN] + jnp.where(sky > 0, hx9[...], 0.0)
         pltpu.make_async_copy(sb9.at[me], rx9.at[mine], to9_recv).start()
 
-        def send(d, carry):
-            to = lax.rem(me + d, CHAN)
-            remote(sb9.at[to], rx9.at[mine], to9_send, to9_recv, (sky, to)).start()
-            return carry
-
-        lax.fori_loop(1, CHAN, send, 0)
+        to_all([(lambda to: sb9.at[to], rx9.at[mine], to9_send, to9_recv, sky)])
 
     is_zero = lax.broadcasted_iota(jnp.int32, (H, 128), 0) == 0
 
@@ -320,6 +355,12 @@
         scale = wsum[me] + jnp.where(sky > 0, hw[...], 0.0) + COMBINE_FLOOR
         rows = lax.broadcasted_iota(jnp.int32, (8, 128), 0)
         scale = 1.0 / jnp.sum(jnp.where(rows == 2 * s, scale, 0.0), axis=0, keepdims=True)
+
+        @pl.when(among(s, STRAIGHT_UP))
+        def _():
+            pltpu.make_async_copy(rx_up.at[s], rx_up.at[s], up_recv.at[s]).wait()
+            rx[s] += jnp.where(sky > 0, rx_up[s], 0.0)
+
         for q in range(2):
             columns = slice(128 * q, 128 * q + 128)
             flat[:MAIN, columns] = rx[s, :, pl.ds(q, 8, stride=2), :].reshape(MAIN, 128) * scale
@@ -353,13 +394,17 @@
             bk[s, :, pl.ds(q, 8, stride=2), :] = rest[:MAIN, columns].reshape(CHAN, 8, 128)
             bk9[pl.ds(2 * s + q, CHAN, stride=8), :] = rest[MAIN:, columns]
         pltpu.make_async_copy(bk.at[s, me], res.at[me, s], back_recv.at[s]).start()
-
-        def send(d, carry):
-            to = lax.rem(me + d, CHAN)
-            remote(bk.at[s, to], res.at[me, s], back_send.at[s], back_recv.at[s], (sky, to)).start()
-            return carry
-
-        lax.fori_loop(1, CHAN, send, 0)
+        straight = among(s, STRAIGHT_DOWN)
+        own = (lambda to: bk.at[s, to], res.at[me, s], back_send.at[s], back_recv.at[s], sky)
+
+        @pl.when(straight)
+        def _():
+            remote(bk.at[s, me], res.at[CHAN + me, s], down_send.at[s], down_recv.at[s], (down, me)).start()
+            to_all([(lambda to: bk.at[s, to], res.at[CHAN + me, s], down_send.at[s], down_recv.at[s], down), own])
+
+        @pl.when(jnp.logical_not(straight))
+        def _():
+            to_all([own])
 
         lanes = pl.ds(pl.multiple_of(s * 128, 128), 128)
         depth[0, 0:H, lanes] = model_re[H:]
@@ -378,14 +423,19 @@
 
     def send_back9():
         pltpu.make_async_copy(bk9.at[mine], res9.at[me], back9_recv).start()
-
-        def send(d, carry):
-            to = lax.rem(me + d, CHAN)
-            row = pl.ds(pl.multiple_of(to * 8, 8), 8)
-            remote(bk9.at[row], res9.at[me], back9_send, back9_recv, (sky, to)).start()
-            return carry
-
-        lax.fori_loop(1, CHAN, send, 0)
+        remote(bk9.at[mine], res9.at[CHAN + me], down9_send, down9_recv, (down, me)).start()
+
+        def row(to):
+            return bk9.at[pl.ds(pl.multiple_of(to * 8, 8), 8)]
+
+        to_all([
+            (row, res9.at[CHAN + me], down9_send, down9_recv, down),
+            (row, res9.at[me], back9_send, back9_recv, sky),
+        ])
+
+    for s in STRAIGHT_UP:
+        straight_own(s)
+    pl.semaphore_wait(ready, 1)
 
     def step(i, carry):
         @pl.when(i < CHUNKS)
@@ -398,6 +448,11 @@
 
         @pl.when(i == 1)
         def _():
+            for s in STRAIGHT_UP:
+                straight_up(s)
+
+        @pl.when(i == 1)
+        def _():
             pltpu.make_async_copy(rx9, rx9, to9_recv).wait()
 
         @pl.when((i >= 1) & (i <= CHUNKS))
@@ -408,7 +463,7 @@
         def _():
             send_back9()
 
-        @pl.when(i >= 2)
+        @pl.when((i >= 2) & jnp.logical_not(among(i - 2, STRAIGHT_DOWN)))
         def _():
             s = i - 2
             pltpu.make_async_copy(bk.at[s], bk.at[s], back_recv.at[s]).wait()
@@ -417,31 +472,27 @@
         return carry
 
     lax.fori_loop(0, CHUNKS + 2, step, 0)
-    pltpu.make_async_copy(hx9, hx9, back9_recv).wait()
-    down_9.start()
-
-    others = pl.ds(0, CHAN - 1)
+
+    for s in range(CHUNKS):
+        for buffer, sem in ((num, up_send), (res, down_send)):
+            pltpu.make_async_copy(buffer.at[second, s], buffer.at[second, s], sem.at[s]).wait()
+        for sem in (to_send, back_send):
+            pltpu.make_async_copy(sb.at[s, all_sent], sb.at[s, all_sent], sem.at[s]).wait()
+        if s in STRAIGHT_DOWN:
+            pltpu.make_async_copy(bk.at[s], bk.at[s], back_recv.at[s]).wait()
+        pltpu.make_async_copy(res.at[second, s], res.at[second, s], down_recv.at[s]).wait()
     up_w.wait_send()
     up_9.wait_send()
-    for s in range(CHUNKS):
-        up_copy(s).wait_send()
-        pltpu.make_async_copy(sb.at[s, others], sb.at[s, others], to_send.at[s]).wait()
-        pltpu.make_async_copy(sb.at[s, others], sb.at[s, others], back_send.at[s]).wait()
-    pltpu.make_async_copy(sb9.at[others], sb9.at[others], to9_send).wait()
-    pltpu.make_async_copy(sb9.at[others], sb9.at[others], back9_send).wait()
-    for s in range(CHUNKS):
-        down_copy(s).wait()
-    down_9.wait()
+    for sem in (to9_send, back9_send):
+        pltpu.make_async_copy(sb9.at[all_sent], sb9.at[all_sent], sem).wait()
+    for sem in (back9_recv, down9_send, down9_recv):
+        pltpu.make_async_copy(hx9, hx9, sem).wait()
 
 
 def body(beam_images, beam_weights, offsets):
     synth, forward, turn = tables()
-    sky = lax.axis_index("sky")
-    start = offsets - sky * (CHAN * F)
-    end = jnp.where(sky == SKY - 1, CHAN * CHUNKS, 2 * CHAN * CHUNKS)
-    start = jnp.concatenate([start, jnp.broadcast_to(end, (1,)).astype(jnp.int32)])
     images = beam_images.reshape(4, 2, PER, 128, 128).transpose(0, 2, 3, 1, 4).reshape(4, PER, 256, 128)
-    weights = beam_weights.reshape(4, 128, 128)
+    weights = beam_weights.reshape(4, 128, 128).transpose(1, 0, 2).reshape(512, 128)
     shape = jax.ShapeDtypeStruct
 
     num, num9, wsum = pl.pallas_call(
@@ -452,7 +503,7 @@
             in_specs=[
                 pl.BlockSpec((1, 8, 256, 128), lambda b, _: (b, 0, 0, 0)),
                 pl.BlockSpec((1, 1, 256, 128), lambda b, _: (b, 8, 0, 0)),
-                pl.BlockSpec((1, 128, 128), lambda b, _: (b, 0, 0)),
+                pl.BlockSpec((512, 128), lambda b, _: (0, 0)),
             ],
             out_specs=[
                 pl.BlockSpec((256, 16, 128), lambda b, _: (0, 0, 0)),
@@ -462,7 +513,7 @@
         ),
         out_shape=[shape((256, 16, 128), F32), shape((64, 8, 128), F32), shape((64, 8, 128), F32)],
         compiler_params=pltpu.CompilerParams(vmem_limit_bytes=VMEM_LIMIT),
-    )(start, images, images, weights)
+    )(offsets, images, images, weights)
 
     dma = pltpu.SemaphoreType.DMA
     vmem = pltpu.VMEM
@@ -483,6 +534,7 @@
             vmem((CHUNKS, CHAN, 16, 128), F32),
             vmem((CHAN, 8, 128), F32),
             vmem((CHUNKS, CHAN, 16, 128), F32),
+            vmem((CHUNKS, CHAN, 16, 128), F32),
             vmem((CHAN * 8, 128), F32),
             vmem((CHUNKS, CHAN, 16, 128), F32),
             vmem((CHAN * 8, 128), F32),
@@ -495,11 +547,12 @@
             dma((CHUNKS,)), dma((CHUNKS,)), dma, dma,
             dma((CHUNKS,)), dma((CHUNKS,)), dma, dma,
             dma((CHUNKS,)), dma((CHUNKS,)), dma, dma,
+            pltpu.SemaphoreType.REGULAR,
         ],
         compiler_params=pltpu.CompilerParams(collective_id=0, has_side_effects=True, vmem_limit_bytes=VMEM_LIMIT),
     )(num.reshape(2 * CHAN, CHUNKS, 16, 128), num9, wsum, jnp.asarray(synth), jnp.asarray(forward), jnp.asarray(turn))
 
-    out = pl.pallas_call(
+    out, depth = pl.pallas_call(
         gather_kernel,
         grid_spec=pltpu.PrefetchScalarGridSpec(
             num_scalar_prefetch=1,
@@ -507,13 +560,17 @@
             in_specs=[
                 pl.BlockSpec((256, 16, 128), lambda b, _: (0, 0, 0)),
                 pl.BlockSpec((64, 8, 128), lambda b, _: (0, 0, 0)),
-                pl.BlockSpec((1, 128, 128), lambda b, _: (b, 0, 0)),
+                pl.BlockSpec((512, 128), lambda b, _: (0, 0)),
+                pl.BlockSpec((2, F // 4, F), lambda b, _: (0, b, 0)),
             ],
-            out_specs=pl.BlockSpec((1, PER, 256, 128), lambda b, _: (b, 0, 0, 0)),
+            out_specs=[
+                pl.BlockSpec((1, PER, 256, 128), lambda b, _: (b, 0, 0, 0)),
+                pl.BlockSpec((2, F // 4, F), lambda b, _: (0, b, 0)),
+            ],
         ),
-        out_shape=shape((BEAMS_DEV, PER, 256, 128), F32),
+        out_shape=[shape((BEAMS_DEV, PER, 256, 128), F32), shape((2, F, F), F32)],
         compiler_params=pltpu.CompilerParams(vmem_limit_bytes=VMEM_LIMIT),
-    )(start, res.reshape(256, 16, 128), res9, weights)
+    )(offsets, res.reshape(256, 16, 128), res9, weights, depth)
     out = out.reshape(4, PER, 128, 2, 128).transpose(0, 3, 1, 2, 4).reshape(4, 2, PER, 128 * 128)
     return out, depth
 

time: 96.3 us -> 85.2 us (0.88)
  Pallas kernels: 91.2 us -> 84.4 us
  local copies, waits for them, and re-layouts: 2.98 us -> 0 us
  other arithmetic: 1.24 us -> 0 us
    pallas_call x1, Pallas kernels: 9.97 us -> 6.58 us  [body(): pl.pallas_call(combine_kernel, grid_spec=pltpu.PrefetchScalarGridSpec(num...]
    unnamed x4 -> x0, local copies, waits for them, and re-layouts: 2.98 us -> none
    pallas_call x1, Pallas kernels: 9.78 us -> 7.51 us  [body(): pl.pallas_call(gather_kernel, grid_spec=pltpu.PrefetchScalarGridSpec(num_...]
    pallas_call x1, Pallas kernels: 71.4 us -> 70.3 us  [body(): pl.pallas_call(exchange_kernel, in_specs=[whole] * 6, out_specs=[whole] *...]
where the time goes in v1:
time: 85.2 us; the launch traced here: 85 us
  Pallas kernels  84.4 us (99%)
    pallas_call x1, Pallas kernels, body(): pl.pallas_call(exchange_kernel, in_specs=[whole] * 6, out_specs=[whole] *...  70.3 us
    pallas_call x1, Pallas kernels, body(): pl.pallas_call(gather_kernel, grid_spec=pltpu.PrefetchScalarGridSpec(num_...  7.51 us
    pallas_call x1, Pallas kernels, body(): pl.pallas_call(combine_kernel, grid_spec=pltpu.PrefetchScalarGridSpec(num...  6.58 us

profile of v1, /device:TPU:1, one launch (start us, length us, event | category | flops | bytes accessed | tf_op | source)
XLA Modules:
  0.0 85.0 jit_solution(11171834728936709715)
XLA Ops:
  0.6 6.6 %shard_map.77 = (f32[256,16,128]{2,1,0:T(8,128)}, f32[64,8,128]{2,1,0:T(8,128)}, f32[64,8,128]{2,1,0:T(8,128)}) custom-call(s32[4]{0:T(128)} %offsets_ref.3, f32[4,9,256,128]{3,2,1,0:T(8,128)} %bitcast.17, f32[4,9,256,128]{3,2,1,0:T(8,128)} %bitcast.18, f32[512,128]{1,0:T(8,128)} %bitcast.21), custom_call_target="tpu_custom_call" | custom-call | tf_op jit(solution)/shard_map/pallas_call | solution.py:498
  7.2 70.3 %shard_map.78 = (f32[64,4,16,128]{3,2,1,0:T(8,128)}, f32[64,8,128]{2,1,0:T(8,128)}, f32[2,512,512]{2,1,0:T(8,128)}) custom-call(f32[64,4,16,128]{3,2,1,0:T(8,128)} %bitcast.20, f32[64,8,128]{2,1,0:T(8,128)} %get-tuple-element.11.num9, f32[64,8,128]{2,1,0:T(8,128)} %get-tuple-element.12.wsum, bf16[520,864]{1,0:T(8,128)(2,1)} %constant.6.clone.synth, ...), custom_call_target="tpu_custom_call" | custom-call | tf_op jit(solution)/shard_map/pallas_call | solution.py:521
  77.5 7.5 %shard_map.79 = (f32[4,9,256,128]{3,2,1,0:T(8,128)}, f32[2,512,512]{2,1,0:T(8,128)}) custom-call(s32[4]{0:T(128)} %offsets_ref.3, f32[256,16,128]{2,1,0:T(8,128)} %bitcast.19, f32[64,8,128]{2,1,0:T(8,128)} %get-tuple-element.14.r9_ref, f32[512,128]{1,0:T(8,128)} %bitcast.22, f32[2,512,512]{2,1,0:T(8,128)} %get-tuple-element.15.d_ref), custom_call_target="tpu_custom_call" | custom-call | tf_op jit(solution)/shard_map/pallas_call | solution.py:555

commit v2 on v1

--- a/solution.py
+++ b/solution.py
@@ -66,6 +66,10 @@
     turn[np.arange(H), (-np.arange(H)) % H] = 1.0
     turn = np.concatenate([turn] * 3, 1).astype(ml_dtypes.bfloat16)
     return synth, forward, turn
+
+
+def pin(value):
+    return pltpu.with_memory_space_constraint(value, pltpu.HBM)
 
 
 def split(value):
@@ -512,8 +516,8 @@
             ],
         ),
         out_shape=[shape((256, 16, 128), F32), shape((64, 8, 128), F32), shape((64, 8, 128), F32)],
-        compiler_params=pltpu.CompilerParams(vmem_limit_bytes=VMEM_LIMIT),
-    )(offsets, images, images, weights)
+        compiler_params=pltpu.CompilerParams(vmem_limit_bytes=14 << 20),
+    )(pin(offsets), pin(images), pin(images), pin(weights))
 
     dma = pltpu.SemaphoreType.DMA
     vmem = pltpu.VMEM
@@ -549,7 +553,7 @@
             dma((CHUNKS,)), dma((CHUNKS,)), dma, dma,
             pltpu.SemaphoreType.REGULAR,
         ],
-        compiler_params=pltpu.CompilerParams(collective_id=0, has_side_effects=True, vmem_limit_bytes=VMEM_LIMIT),
+        compiler_params=pltpu.CompilerParams(collective_id=0, has_side_effects=True, vmem_limit_bytes=30 << 20),
     )(num.reshape(2 * CHAN, CHUNKS, 16, 128), num9, wsum, jnp.asarray(synth), jnp.asarray(forward), jnp.asarray(turn))
 
     out, depth = pl.pallas_call(
@@ -569,7 +573,7 @@
             ],
         ),
         out_shape=[shape((BEAMS_DEV, PER, 256, 128), F32), shape((2, F, F), F32)],
-        compiler_params=pltpu.CompilerParams(vmem_limit_bytes=VMEM_LIMIT),
+        compiler_params=pltpu.CompilerParams(vmem_limit_bytes=18 << 20),
     )(offsets, res.reshape(256, 16, 128), res9, weights, depth)
     out = out.reshape(4, PER, 128, 2, 128).transpose(0, 3, 1, 2, 4).reshape(4, 2, PER, 128 * 128)
     return out, depth

time: 85.2 us -> 77.6 us (0.911)
  Pallas kernels: 84.4 us -> 76.7 us
    pallas_call x1, Pallas kernels: 70.3 us -> 66.3 us  [body(): pl.pallas_call(exchange_kernel, in_specs=[whole] * 6, out_specs=[whole] *...]
    pallas_call x1, Pallas kernels: 7.51 us -> 5.13 us  [body(): pl.pallas_call(gather_kernel, grid_spec=pltpu.PrefetchScalarGridSpec(num_...]
    pallas_call x1, Pallas kernels: 6.58 us -> 5.29 us  [body(): pl.pallas_call(combine_kernel, grid_spec=pltpu.PrefetchScalarGridSpec(num...]
where the time goes in v2:
time: 77.6 us; the launch traced here: 77.4 us
  Pallas kernels  76.7 us (99%)
    pallas_call x1, Pallas kernels, body(): pl.pallas_call(exchange_kernel, in_specs=[whole] * 6, out_specs=[whole] *...  66.3 us
    pallas_call x1, Pallas kernels, body(): pl.pallas_call(combine_kernel, grid_spec=pltpu.PrefetchScalarGridSpec(num...  5.29 us
    pallas_call x1, Pallas kernels, body(): pl.pallas_call(gather_kernel, grid_spec=pltpu.PrefetchScalarGridSpec(num_...  5.13 us

profile of v2, /device:TPU:1, one launch (start us, length us, event | category | flops | bytes accessed | tf_op | source)
XLA Modules:
  0.0 77.4 jit_solution(1386776240653262142)
XLA Ops:
  0.6 0.0 copy-start.1
  0.6 0.0 copy-start.2
  0.7 0.0 copy-start.3
  0.7 5.3 %shard_map.77 = (f32[256,16,128]{2,1,0:T(8,128)S(1)}, f32[64,8,128]{2,1,0:T(8,128)S(1)}, f32[64,8,128]{2,1,0:T(8,128)S(1)}) custom-call(s32[4]{0:T(128)} %offsets_ref.3, f32[4,9,256,128]{3,2,1,0:T(8,128)} %bitcast.21, f32[4,9,256,128]{3,2,1,0:T(8,128)} %bitcast.22, f32[512,128]{1,0:T(8,128)} %bitcast.19), custom_call_target="tpu_custom_call" | custom-call | tf_op jit(solution)/shard_map/pallas_call | solution.py:502
  6.0 0.0 copy-done.1
  6.0 0.0 copy-done.2
  6.0 0.0 copy-done.3
  6.0 0.0 copy-start
  6.0 0.0 copy-start.4
  6.0 66.3 %shard_map.78 = (f32[64,4,16,128]{3,2,1,0:T(8,128)S(1)}, f32[64,8,128]{2,1,0:T(8,128)S(1)}, f32[2,512,512]{2,1,0:T(8,128)S(1)}) custom-call(f32[64,4,16,128]{3,2,1,0:T(8,128)S(1)} %bitcast.18, f32[64,8,128]{2,1,0:T(8,128)S(1)} %get-tuple-element.11.num9, f32[64,8,128]{2,1,0:T(8,128)S(1)} %get-tuple-element.12.wsum, bf16[520,864]{1,0:T(8,128)(2,1)S(1)} %copy-done.1, ...), custom_call_target="tpu_custom_call" | custom-call | tf_op jit(solution)/shard_map/pallas_call | solution.py:525
  72.3 0.0 copy-done
  72.3 0.0 copy-done.4
  72.3 5.1 %shard_map.79 = (f32[4,9,256,128]{3,2,1,0:T(8,128)}, f32[2,512,512]{2,1,0:T(8,128)}) custom-call(s32[4]{0:T(128)S(1)} %copy-done.4, f32[256,16,128]{2,1,0:T(8,128)S(1)} %bitcast.17, f32[64,8,128]{2,1,0:T(8,128)S(1)} %get-tuple-element.14.r9_ref, f32[512,128]{1,0:T(8,128)S(1)} %bitcast.20, f32[2,512,512]{2,1,0:T(8,128)S(1)} %get-tuple-element.15.d_ref), custom_call_target="tpu_custom_call" | custom-call | tf_op jit(solution)/shard_map/pallas_call | solution.py:559
Async XLA Ops:
  0.6 5.3 %copy-start.1 = (bf16[520,864]{1,0:T(8,128)(2,1)S(1)}, bf16[520,864]{1,0:T(8,128)(2,1)}, u32[]{:S(2)}) copy-start(bf16[520,864]{1,0:T(8,128)(2,1)} %constant.6.clone.synth) | copy-start | bytes 2695684
  0.6 5.3 %copy-start.2 = (bf16[288,1536]{1,0:T(8,128)(2,1)S(1)}, bf16[288,1536]{1,0:T(8,128)(2,1)}, u32[]{:S(2)}) copy-start(bf16[288,1536]{1,0:T(8,128)(2,1)} %constant.7.clone.forward) | copy-start | bytes 2654212
  0.7 5.3 %copy-start.3 = (bf16[256,768]{1,0:T(8,128)(2,1)S(1)}, bf16[256,768]{1,0:T(8,128)(2,1)}, u32[]{:S(2)}) copy-start(bf16[256,768]{1,0:T(8,128)(2,1)} %constant.8.clone.turn) | copy-start | bytes 1179652
  6.0 66.3 %copy-start = (f32[4,16384]{1,0:T(4,128)S(1)}, f32[4,16384]{1,0:T(4,128)}, u32[]{:S(2)}) copy-start(f32[4,16384]{1,0:T(4,128)} %param.7) | copy-start | bytes 786436
  6.0 66.3 %copy-start.4 = (s32[4]{0:T(128)S(1)}, s32[4]{0:T(128)}, u32[]{:S(2)}) copy-start(s32[4]{0:T(128)} %offsets_ref.3) | copy-start | bytes 52

commit v3 on v2

--- a/solution.py
+++ b/solution.py
@@ -32,7 +32,7 @@
 F32 = jnp.float32
 BF16 = jnp.bfloat16
 VMEM_LIMIT = 56 << 20
-UNROLL = 8
+UNROLL = 16
 STRAIGHT_UP = ()
 STRAIGHT_DOWN = (3,)
 

time: 77.6 us -> 76.7 us (0.988)
  Pallas kernels: 76.7 us -> 75.8 us
where the time goes in v3:
time: 76.7 us; the launch traced here: 76.6 us
  Pallas kernels  75.8 us (99%)
    pallas_call x1, Pallas kernels, body(): pl.pallas_call(exchange_kernel, in_specs=[whole] * 6, out_specs=[whole] *...  66.3 us
    pallas_call x1, Pallas kernels, body(): pl.pallas_call(combine_kernel, grid_spec=pltpu.PrefetchScalarGridSpec(num...  4.97 us
    pallas_call x1, Pallas kernels, body(): pl.pallas_call(gather_kernel, grid_spec=pltpu.PrefetchScalarGridSpec(num_...  4.59 us

profile of v3, /device:TPU:1, one launch (start us, length us, event | category | flops | bytes accessed | tf_op | source)
XLA Modules:
  0.0 76.6 jit_solution(14425795341734179330)
XLA Ops:
  0.6 0.0 copy-start.1
  0.6 0.0 copy-start.2
  0.7 0.0 copy-start.3
  0.7 5.0 %shard_map.77 = (f32[256,16,128]{2,1,0:T(8,128)S(1)}, f32[64,8,128]{2,1,0:T(8,128)S(1)}, f32[64,8,128]{2,1,0:T(8,128)S(1)}) custom-call(s32[4]{0:T(128)} %offsets_ref.3, f32[4,9,256,128]{3,2,1,0:T(8,128)} %bitcast.21, f32[4,9,256,128]{3,2,1,0:T(8,128)} %bitcast.22, f32[512,128]{1,0:T(8,128)} %bitcast.19), custom_call_target="tpu_custom_call" | custom-call | tf_op jit(solution)/shard_map/pallas_call | solution.py:502
  5.6 0.0 copy-done.1
  5.7 0.0 copy-done.2
  5.7 0.0 copy-done.3
  5.7 0.0 copy-start
  5.7 0.0 copy-start.4
  5.7 66.3 %shard_map.78 = (f32[64,4,16,128]{3,2,1,0:T(8,128)S(1)}, f32[64,8,128]{2,1,0:T(8,128)S(1)}, f32[2,512,512]{2,1,0:T(8,128)S(1)}) custom-call(f32[64,4,16,128]{3,2,1,0:T(8,128)S(1)} %bitcast.18, f32[64,8,128]{2,1,0:T(8,128)S(1)} %get-tuple-element.11.num9, f32[64,8,128]{2,1,0:T(8,128)S(1)} %get-tuple-element.12.wsum, bf16[520,864]{1,0:T(8,128)(2,1)S(1)} %copy-done.1, ...), custom_call_target="tpu_custom_call" | custom-call | tf_op jit(solution)/shard_map/pallas_call | solution.py:525
  72.0 0.0 copy-done
  72.0 0.0 copy-done.4
  72.0 4.6 %shard_map.79 = (f32[4,9,256,128]{3,2,1,0:T(8,128)}, f32[2,512,512]{2,1,0:T(8,128)}) custom-call(s32[4]{0:T(128)S(1)} %copy-done.4, f32[256,16,128]{2,1,0:T(8,128)S(1)} %bitcast.17, f32[64,8,128]{2,1,0:T(8,128)S(1)} %get-tuple-element.14.r9_ref, f32[512,128]{1,0:T(8,128)S(1)} %bitcast.20, f32[2,512,512]{2,1,0:T(8,128)S(1)} %get-tuple-element.15.d_ref), custom_call_target="tpu_custom_call" | custom-call | tf_op jit(solution)/shard_map/pallas_call | solution.py:559
Async XLA Ops:
  0.6 5.0 %copy-start.1 = (bf16[520,864]{1,0:T(8,128)(2,1)S(1)}, bf16[520,864]{1,0:T(8,128)(2,1)}, u32[]{:S(2)}) copy-start(bf16[520,864]{1,0:T(8,128)(2,1)} %constant.6.clone.synth) | copy-start | bytes 2695684
  0.6 5.0 %copy-start.2 = (bf16[288,1536]{1,0:T(8,128)(2,1)S(1)}, bf16[288,1536]{1,0:T(8,128)(2,1)}, u32[]{:S(2)}) copy-start(bf16[288,1536]{1,0:T(8,128)(2,1)} %constant.7.clone.forward) | copy-start | bytes 2654212
  0.7 5.0 %copy-start.3 = (bf16[256,768]{1,0:T(8,128)(2,1)S(1)}, bf16[256,768]{1,0:T(8,128)(2,1)}, u32[]{:S(2)}) copy-start(bf16[256,768]{1,0:T(8,128)(2,1)} %constant.8.clone.turn) | copy-start | bytes 1179652
  5.7 66.3 %copy-start = (f32[4,16384]{1,0:T(4,128)S(1)}, f32[4,16384]{1,0:T(4,128)}, u32[]{:S(2)}) copy-start(f32[4,16384]{1,0:T(4,128)} %param.7) | copy-start | bytes 786436
  5.7 66.3 %copy-start.4 = (s32[4]{0:T(128)S(1)}, s32[4]{0:T(128)}, u32[]{:S(2)}) copy-start(s32[4]{0:T(128)} %offsets_ref.3) | copy-start | bytes 52
